TPU v7x, 256 devices: a whole 4x4x8 slice. The times are simulated.
256 devices in a mesh: expert: 32 (over x, y, core), shard: 8 (over z).
Axes of the slice: x: 4, y: 4, z: 8, core: 2. Of those that a mesh axis runs over, the one named last changes fastest.
Arguments:
- head_outputs: bfloat16 [32768, 1024], P(('expert', 'shard')), may hold values from -6 to 6
- residual: bfloat16 [32768, 1024], P(('expert', 'shard')), may hold values from -4 to 4
- output_weight: bfloat16 [1024, 1024], P('shard'), may hold values from -0.1875 to 0.1875
- router: bfloat16 [1024, 32], replicated, may hold values from -0.095703125 to 0.095703125
- norm_gain: float32 [1024], replicated, may hold values from 0.1 to 1.9
- placed_gate_up: bfloat16 [64, 1024, 1024], P('expert', 'shard'), may hold values from -0.1875 to 0.1875
- placed_down: bfloat16 [64, 512, 1024], P('expert', 'shard'), may hold values from -0.25 to 0.25
- routes: int32 [32768, 8], P(('expert', 'shard')), may hold values from 0 to 31, all different within a row; in each aligned block of 128 rows (0 to 127, 128 to 255, ...) at most 48 rows name the same one
- replica_pick: int32 [32768, 8], P(('expert', 'shard')), may hold values from 0 to 5
- placement: int32 [64], replicated, may hold values from 0 to 31, as said below
- final_gain: float32 [1024], replicated, may hold values from 0.1 to 1.9
Outputs:
- next_input: bfloat16 [32768, 1024], P(('expert', 'shard'))
Inputs may be any that keep to these rules, and one draw needn't show every extreme that they name: `routes`: each token names 8 different experts. Among the 128 tokens of one device no expert is named more than 48 times, and in some device's tokens one expert is named exactly 48 times. `placement`: every expert holds one to three of the 64 placements: a quarter of the experts hold three, half of them two, the rest one.
All inputs are finite; a program needn't handle non-finite values.
Results may differ from a plain program's by a relative error of at most 0.011.
Values may be sent and summed in bfloat16 or wider, within the bound.
A program may use at most 128 MiB of HBM per device.

v0:
```python
import math
import jax
import jax.numpy as jnp
from jax import lax
from jax.sharding import PartitionSpec as P

CAP = 48
eps_norm = 1e-06
most_copies = 3


def rms_scale(values, scale_gain):
    mean_square = jnp.mean(values * values, axis=-1, keepdims=True)
    return values * lax.rsqrt(mean_square + eps_norm) * scale_gain


def choose_slots(routes, replica_pick, placement, experts):
    labels = jnp.arange(experts, dtype=jnp.int32)
    holder_mask = (placement[None, :] == labels[:, None]).astype(jnp.int32)
    before = jnp.cumsum(holder_mask, axis=1) - holder_mask
    copies = jnp.sum(holder_mask, axis=1)
    places = jnp.arange(placement.shape[0], dtype=jnp.int32)
    route_hits = (routes[..., None] == labels).astype(jnp.int32)
    held_count = jnp.sum(route_hits * copies, axis=-1)
    wanted = replica_pick % held_count
    chosen = jnp.zeros(routes.shape, jnp.int32)
    for replica in range(most_copies):
        column = jnp.sum(
            holder_mask * (before == replica).astype(jnp.int32) * places[None, :], axis=1
        )
        candidate = jnp.sum(route_hits * column, axis=-1)
        chosen = jnp.where(wanted == replica, candidate, chosen)
    return chosen


def padded_experts(inbound, gate_up, down_proj):
    sources, slot_count, slot_depth, model_width = inbound.shape
    per_source = slot_count * slot_depth
    upper_bound = max(1, 1024 // per_source)
    power_two = 1 << upper_bound.bit_length() - 1
    group_size = math.gcd(sources, power_two)
    stacked = inbound.reshape(
        sources // group_size, group_size, slot_count, slot_depth, model_width
    )
    hidden_units = down_proj.shape[1]

    def apply_block(block_part):
        both_parts = jnp.einsum(
            "bjmd,jdf->bjmf", block_part, gate_up, preferred_element_type=jnp.float32
        )
        activated = (
            jax.nn.silu(both_parts[..., :hidden_units]) * both_parts[..., hidden_units:]
        ).astype(jnp.bfloat16)
        return jnp.einsum(
            "bjmf,jfd->bjmd", activated, down_proj, preferred_element_type=jnp.float32
        ).astype(jnp.bfloat16)

    return lax.map(apply_block, stacked).reshape(inbound.shape)


def body(
    head_outputs,
    residual,
    output_weight,
    router,
    norm_gain,
    placed_gate_up,
    placed_down,
    routes,
    replica_pick,
    placement,
    final_gain,
):
    row_count, model_width = residual.shape
    route_count = routes.shape[1]
    experts = router.shape[1]
    place_count = placement.shape[0]
    groups = lax.axis_size("expert")
    slot_count = place_count // groups
    capacity = CAP
    projected = jnp.dot(
        head_outputs,
        lax.all_gather(output_weight, "shard", axis=0, tiled=True),
        preferred_element_type=jnp.float32,
    )
    hidden = (residual.astype(jnp.float32) + projected).astype(jnp.bfloat16)
    hidden_wide = hidden.astype(jnp.float32)
    normed = rms_scale(hidden_wide, norm_gain).astype(jnp.bfloat16)
    logits = jnp.dot(normed, router, preferred_element_type=jnp.float32)
    labels = jnp.arange(experts, dtype=jnp.int32)
    selector = (routes[..., None] == labels).astype(jnp.float32)
    chosen_logits = jnp.sum(selector * logits[:, None, :], axis=-1)
    raised = jnp.exp(chosen_logits)
    route_weight = raised / jnp.sum(raised, axis=-1, keepdims=True)
    slot_ids = choose_slots(routes, replica_pick, placement, experts).reshape(-1)
    slot_hits = (slot_ids[:, None] == jnp.arange(place_count, dtype=jnp.int32)).astype(jnp.int32)
    slot_rank = jnp.sum((jnp.cumsum(slot_hits, axis=0) - slot_hits) * slot_hits, axis=1)
    copies_out = jnp.repeat(normed, route_count, axis=0)
    gate_up, down_proj = (
        lax.all_gather(placed_gate_up, "shard", axis=1, tiled=True),
        lax.all_gather(placed_down, "shard", axis=1, tiled=True),
    )
    buffer_index = slot_ids * capacity + slot_rank
    outbound = (
        jnp.zeros((place_count * capacity, model_width), jnp.bfloat16)
        .at[buffer_index]
        .set(copies_out)
    )
    inbound = lax.all_to_all(
        outbound.reshape(groups, slot_count * capacity, model_width),
        "expert",
        split_axis=0,
        concat_axis=0,
        tiled=True,
    )
    inbound = inbound.reshape(groups, slot_count, capacity, model_width)
    answers = padded_experts(inbound, gate_up, down_proj)
    returned = lax.all_to_all(
        answers.reshape(groups, slot_count * capacity, model_width),
        "expert",
        split_axis=0,
        concat_axis=0,
        tiled=True,
    )
    returned = returned.reshape(place_count * capacity, model_width)
    gathered = returned[buffer_index].reshape(row_count, route_count, model_width)
    mixture = jnp.sum(route_weight[..., None] * gathered.astype(jnp.float32), axis=1)
    return rms_scale(hidden_wide + mixture, final_gain).astype(jnp.bfloat16)


def solution(mesh):
    return jax.shard_map(
        body,
        mesh=mesh,
        in_specs=(
            P(("expert", "shard"), None),
            P(("expert", "shard"), None),
            P("shard", None),
            P(),
            P(),
            P("expert", "shard", None),
            P("expert", "shard", None),
            P(("expert", "shard"), None),
            P(("expert", "shard"), None),
            P(),
            P(),
        ),
        out_specs=P(("expert", "shard"), None),
        check_vma=False,
    )
```

profile of v0, /device:TPU:8, one launch (start us, length us, event | category | flops | bytes accessed | tf_op | source)
XLA Modules:
  0.0 298.7 jit_solution(8808641445974317560)
XLA Ops:
  6.5 0.7 all-gather.4.cloned.1.call-update
  7.3 0.7 all-gather.8.cloned.1.call-update
  8.1 0.7 all-gather.6.cloned.1.call-update
  8.7 0.7 fusion.34
  9.4 0.2 reduce_window_sum.26
  9.6 0.8 fusion.33
  10.4 0.8 select_reduce_fusion.3
  11.3 0.8 broadcast_multiply_fusion
  12.1 0.1 copy.25
  12.2 0.1 eq.111
  12.3 0.1 eq.107
  12.4 0.1 copy.24
  12.5 0.1 mul.172
  12.6 18.0 %reduce-window.6 = s32[64,8,128]{2,1,0:T(8,128)S(1)} reduce-window(s32[64,8,128]{2,1,0:T(8,128)S(1)} %fusion.27, s32[]{:T(128)} %copy.53), window={size=1x1x128 pad=0_0x0_0x127_0}, to_apply=%region_12.13 | reduce-window | flops 8323072 | bytes 524292 | tf_op jit(solution)/shard_map/reduce-window
  30.6 0.1 slice.18
  30.8 0.1 copy.27
  30.9 0.1 copy.28
  31.0 0.1 broadcast_add_fusion
  31.2 0.1 fusion.26
  31.3 21.6 %all-gather.4.cloned.1.call-done = bf16[1024,1024]{1,0:T(8,128)(2,1)} async-done(((bf16[128,1024]{1,0:T(8,128)(2,1)}), bf16[1024,1024]{1,0:T(8,128)(2,1)}) %all-gather.4.cloned.1.call-update) | async-done | bytes 2097168 | tf_op jit(solution)/shard_map/all_gather | solution.py:83
  52.9 2.1 multiply_reduce_fusion.1
  55.0 0.1 multiply_convert_fusion.1
  55.2 9.0 %scatter_custom_fusion = bf16[3072,1024]{1,0:T(8,128)(2,1)} fusion(s32[1024]{0:T(1024)S(1)} %bitcast.75, bf16[]{:T(256)} %constant.52.clone.1, bf16[128,1024]{1,0:T(8,128)(2,1)S(1)} %multiply_convert_fusion.1), kind=kCustom, calls=%fused_computation.18 | custom fusion | bytes 6553602 | tf_op jit(solution)/shard_map/scatter | solution.py:107
  64.2 8.2 %all-to-all-start = ((bf16[32,96,1024]{2,1,0:T(8,128)(2,1)}), bf16[32,96,1024]{2,1,0:T(8,128)(2,1)}, u32[]{:S(2)}, u32[]{:S(2)}) async-start(bf16[32,96,1024]{2,1,0:T(8,128)(2,1)} %bitcast.70), calls=%async_computation | async-start | bytes 12582912 | tf_op jit(solution)/shard_map/all_to_all | solution.py:109
  72.4 22.6 %all-gather.8.cloned.1.call-done = bf16[2,512,1024]{2,1,0:T(8,128)(2,1)} async-done(((bf16[2,64,1024]{2,1,0:T(8,128)(2,1)}), bf16[2,512,1024]{2,1,0:T(8,128)(2,1)}) %all-gather.8.cloned.1.call-update) | async-done | bytes 2097168 | tf_op jit(solution)/shard_map/all_gather | solution.py:101
  95.0 55.0 %all-gather.6.cloned.1.call-done = bf16[2,1024,1024]{2,1,0:T(8,128)(2,1)} async-done(((bf16[2,128,1024]{2,1,0:T(8,128)(2,1)}), bf16[2,1024,1024]{2,1,0:T(8,128)(2,1)}) %all-gather.6.cloned.1.call-update) | async-done | bytes 4194320 | tf_op jit(solution)/shard_map/all_gather | solution.py:100
  150.1 9.9 %all-to-all-done = bf16[32,96,1024]{2,1,0:T(8,128)(2,1)} async-done(((bf16[32,96,1024]{2,1,0:T(8,128)(2,1)}), bf16[32,96,1024]{2,1,0:T(8,128)(2,1)}, u32[]{:S(2)}, u32[]{:S(2)}) %all-to-all-start) | async-done | bytes 6291488 | tf_op jit(solution)/shard_map/all_to_all | solution.py:109
  160.0 27.9 %while.10 = (s32[]{:T(128)}, bf16[4,8,2,48,1024]{4,3,2,1,0:T(8,128)(2,1)}, bf16[4,8,2,48,1024]{4,3,2,1,0:T(8,128)(2,1)}, bf16[2,1024,1024]{2,1,0:T(8,128)(2,1)}, bf16[2,512,1024]{2,1,0:T(8,128)(2,1)}, /*index=5*/s32[]{:T(128)}) while((s32[]{:T(128)}, bf16[4,8,2,48,1024]{4,3,2,1,0:T(8,128)(2,1)}, bf16[4,8,2,48,1024]{4,3,2,1,0:T(8,128)(2,1)}, ...), condition=%wide.region_17.18_spmd, body=%wide.region_16.17_spmd.sunk | while | flops 2419064832 | bytes 27263088 | solution.py:58
  160.0 4.6 %fusion.48 = f32[8,2,48,1024]{3,2,0,1:T(8,128)S(1)} fusion(bf16[2,1024,1024]{2,1,0:T(8,128)(2,1)} %get-tuple-element.113, bf16[4,8,2,48,1024]{4,3,2,1,0:T(8,128)(2,1)} %get-tuple-element.112, s32[]{:T(128)S(6)} %copy.48), kind=kOutput, calls=%fused_computation.6.clone.1 | convolution fusion | flops 1610612736 | bytes 8912900 | tf_op jit(solution)/shard_map/while/body/eval_jaxpr/bjmd,jdf->bjmf/dot_general | solution.py:48
  164.6 1.0 fusion.49
  165.6 1.3 copy_dynamic-update-slice_fusion.2
  166.9 4.6 %fusion.48 = f32[8,2,48,1024]{3,2,0,1:T(8,128)S(1)} fusion(bf16[2,1024,1024]{2,1,0:T(8,128)(2,1)} %get-tuple-element.113, bf16[4,8,2,48,1024]{4,3,2,1,0:T(8,128)(2,1)} %get-tuple-element.112, s32[]{:T(128)S(6)} %copy.48), kind=kOutput, calls=%fused_computation.6.clone.1 | convolution fusion | flops 1610612736 | bytes 8912900 | tf_op jit(solution)/shard_map/while/body/eval_jaxpr/bjmd,jdf->bjmf/dot_general | solution.py:48
  171.6 1.0 fusion.49
  172.6 1.4 copy_dynamic-update-slice_fusion.2
  174.0 4.6 %fusion.48 = f32[8,2,48,1024]{3,2,0,1:T(8,128)S(1)} fusion(bf16[2,1024,1024]{2,1,0:T(8,128)(2,1)} %get-tuple-element.113, bf16[4,8,2,48,1024]{4,3,2,1,0:T(8,128)(2,1)} %get-tuple-element.112, s32[]{:T(128)S(6)} %copy.48), kind=kOutput, calls=%fused_computation.6.clone.1 | convolution fusion | flops 1610612736 | bytes 8912900 | tf_op jit(solution)/shard_map/while/body/eval_jaxpr/bjmd,jdf->bjmf/dot_general | solution.py:48
  178.6 1.0 fusion.49
  179.7 1.3 copy_dynamic-update-slice_fusion.2
  181.0 4.6 %fusion.48 = f32[8,2,48,1024]{3,2,0,1:T(8,128)S(1)} fusion(bf16[2,1024,1024]{2,1,0:T(8,128)(2,1)} %get-tuple-element.113, bf16[4,8,2,48,1024]{4,3,2,1,0:T(8,128)(2,1)} %get-tuple-element.112, s32[]{:T(128)S(6)} %copy.48), kind=kOutput, calls=%fused_computation.6.clone.1 | convolution fusion | flops 1610612736 | bytes 8912900 | tf_op jit(solution)/shard_map/while/body/eval_jaxpr/bjmd,jdf->bjmf/dot_general | solution.py:48
  185.6 1.0 fusion.49
  186.6 1.3 copy_dynamic-update-slice_fusion.2
  187.9 5.1 %all-to-all-start.1 = ((bf16[32,96,1024]{2,1,0:T(8,128)(2,1)}), bf16[32,96,1024]{2,1,0:T(8,128)(2,1)}, u32[]{:S(2)}, u32[]{:S(2)}) async-start(bf16[32,96,1024]{2,1,0:T(8,128)(2,1)} %bitcast.71), calls=%async_computation.1 | async-start | bytes 12582912 | tf_op jit(solution)/shard_map/all_to_all | solution.py:118
  193.1 0.2 fusion.35
  193.3 0.1 copy.23
  193.5 87.8 %all-to-all-done.1 = bf16[32,96,1024]{2,1,0:T(8,128)(2,1)} async-done(((bf16[32,96,1024]{2,1,0:T(8,128)(2,1)}), bf16[32,96,1024]{2,1,0:T(8,128)(2,1)}, u32[]{:S(2)}, u32[]{:S(2)}) %all-to-all-start.1) | async-done | bytes 6291488 | tf_op jit(solution)/shard_map/all_to_all | solution.py:118
  281.3 8.6 %gather_fusion = bf16[1024,1024]{1,0:T(8,128)(2,1)S(1)} fusion(bf16[3072,1024]{1,0:T(8,128)(2,1)} %bitcast.16, s32[1024]{0:T(1024)S(1)} %broadcast_clamp_fusion), kind=kCustom, calls=%fused_computation | custom fusion | bytes 4198400 | tf_op jit(solution)/shard_map/gather | solution.py:126
  289.9 1.3 fusion.17
  291.2 0.2 multiply_reduce_fusion
  291.3 0.8 multiply_convert_fusion
  (34 shorter events, 0.3 us)
Async XLA Ops:
  6.5 46.4 %copy-start = (bf16[128,1024]{1,0:T(8,128)(2,1)S(1)}, bf16[128,1024]{1,0:T(8,128)(2,1)}, u32[]{:S(2)}) copy-start(bf16[128,1024]{1,0:T(8,128)(2,1)} %param.13) | copy-start | bytes 786436
  6.5 46.4 %copy-start.1 = (bf16[128,1024]{1,0:T(8,128)(2,1)S(1)}, bf16[128,1024]{1,0:T(8,128)(2,1)}, u32[]{:S(2)}) copy-start(bf16[128,1024]{1,0:T(8,128)(2,1)} %param.14) | copy-start | bytes 786436
  6.5 46.4 %all-gather.4.cloned.1.call-start = ((), (), s32[]{:S(2)}) async-start(), calls=%async_computation.2 | async-start | bytes 2359296 | tf_op jit(solution)/shard_map/all_gather | solution.py:83
  7.3 87.8 %all-gather.8.cloned.1.call-start = ((), (), s32[]{:S(2)}) async-start(), calls=%async_computation.4 | async-start | bytes 2359296 | tf_op jit(solution)/shard_map/all_gather | solution.py:101
  8.0 142.1 %all-gather.6.cloned.1.call-start = ((), (), s32[]{:S(2)}) async-start(), calls=%async_computation.3 | async-start | bytes 4718592 | tf_op jit(solution)/shard_map/all_gather | solution.py:100
  30.7 24.3 %copy-start.4 = (f32[1024]{0:T(1024)S(1)}, f32[1024]{0:T(1024)}, u32[]{:S(2)}) copy-start(f32[1024]{0:T(1024)} %param.17) | copy-start | bytes 12292
  64.2 95.8 %all-to-all-start = ((bf16[32,96,1024]{2,1,0:T(8,128)(2,1)}), bf16[32,96,1024]{2,1,0:T(8,128)(2,1)}, u32[]{:S(2)}, u32[]{:S(2)}) async-start(bf16[32,96,1024]{2,1,0:T(8,128)(2,1)} %bitcast.70), calls=%async_computation | async-start | bytes 12582912 | tf_op jit(solution)/shard_map/all_to_all | solution.py:109
  160.0 4.6 %copy-start.6 = (bf16[2,512,1024]{2,1,0:T(8,128)(2,1)S(1)}, bf16[2,512,1024]{2,1,0:T(8,128)(2,1)}, u32[]{:S(2)}) copy-start(bf16[2,512,1024]{2,1,0:T(8,128)(2,1)} %get-tuple-element.114) | copy-start | bytes 6291460 | tf_op jit(solution)/shard_map/while
  166.9 4.6 %copy-start.6 = (bf16[2,512,1024]{2,1,0:T(8,128)(2,1)S(1)}, bf16[2,512,1024]{2,1,0:T(8,128)(2,1)}, u32[]{:S(2)}) copy-start(bf16[2,512,1024]{2,1,0:T(8,128)(2,1)} %get-tuple-element.114) | copy-start | bytes 6291460 | tf_op jit(solution)/shard_map/while
  174.0 4.6 %copy-start.6 = (bf16[2,512,1024]{2,1,0:T(8,128)(2,1)S(1)}, bf16[2,512,1024]{2,1,0:T(8,128)(2,1)}, u32[]{:S(2)}) copy-start(bf16[2,512,1024]{2,1,0:T(8,128)(2,1)} %get-tuple-element.114) | copy-start | bytes 6291460 | tf_op jit(solution)/shard_map/while
  181.0 4.6 %copy-start.6 = (bf16[2,512,1024]{2,1,0:T(8,128)(2,1)S(1)}, bf16[2,512,1024]{2,1,0:T(8,128)(2,1)}, u32[]{:S(2)}) copy-start(bf16[2,512,1024]{2,1,0:T(8,128)(2,1)} %get-tuple-element.114) | copy-start | bytes 6291460 | tf_op jit(solution)/shard_map/while
  187.9 5.1 %copy-start.2 = (bf16[1024,32]{0,1:T(8,128)(2,1)S(1)}, bf16[1024,32]{0,1:T(8,128)(2,1)}, u32[]{:S(2)}) copy-start(bf16[1024,32]{0,1:T(8,128)(2,1)} %param.16) | copy-start | bytes 196612
  187.9 5.3 %copy-start.3 = (s32[128,8]{0,1:T(8,128)S(1)}, s32[128,8]{0,1:T(8,128)}, u32[]{:S(2)}) copy-start(s32[128,8]{0,1:T(8,128)} %param.20) | copy-start | bytes 12292
  187.9 93.4 %all-to-all-start.1 = ((bf16[32,96,1024]{2,1,0:T(8,128)(2,1)}), bf16[32,96,1024]{2,1,0:T(8,128)(2,1)}, u32[]{:S(2)}, u32[]{:S(2)}) async-start(bf16[32,96,1024]{2,1,0:T(8,128)(2,1)} %bitcast.71), calls=%async_computation.1 | async-start | bytes 12582912 | tf_op jit(solution)/shard_map/all_to_all | solution.py:118
  289.9 1.5 copy-start.5
Sparse Core Ops, SparseCore 0:
  9.2 43.6 all-gather.3
  54.7 40.2 all-gather.7
  96.8 53.1 all-gather.5
where the time goes:
time: 299 us
  waiting for transfers between devices  199 us (67%)
  matrix products  24.8 us (8%)
  other arithmetic  24.1 us (8%)
  local copies, waits for them, and re-layouts  23.9 us (8%)
  starting transfers between devices  13.4 us (4%)
  between operations  13.3 us (4%)
    all_to_all x1, waiting for transfers between devices, body(): lax.all_to_all(answers.reshape(groups, slot_count * capacity, model_width...  87.8 us
    all_gather x1, waiting for transfers between devices, body(): lax.all_gather(placed_gate_up, 'shard', axis=1, tiled=True)  55 us
    all_gather x1, waiting for transfers between devices, body(): lax.all_gather(placed_down, 'shard', axis=1, tiled=True)  22.6 us
    all_gather x1, waiting for transfers between devices, body(): lax.all_gather(output_weight, 'shard', axis=0, tiled=True)  21.6 us
    dot_general x4, matrix products, apply_block(): jnp.einsum('bjmd,jdf->bjmf', block_part, gate_up, preferred_element_type=...  18.4 us
    another operation x3, other arithmetic  18.2 us
    all_to_all x1, waiting for transfers between devices, body(): lax.all_to_all(outbound.reshape(groups, slot_count * capacity, model_widt...  9.92 us
    scatter x1, local copies, waits for them, and re-layouts, body(): outbound = jnp.zeros((place_count * capacity, model_width), jnp.bfloat16)...  9.04 us
  transfers between devices with their start and end apart: 5, of which 5 were waited for; matrix products, arithmetic and copies ran while one was open for 11% of the time, Pallas kernels for 0%

commit v1 on v0

--- a/solution.py
+++ b/solution.py
@@ -7,6 +7,11 @@
 CAP = 48
 eps_norm = 1e-06
 most_copies = 3
+
+
+def all_by_exchange(x, axis, dim):
+    sent = jnp.stack([x] * lax.axis_size(axis))
+    return jnp.concatenate(lax.all_to_all(sent, axis, 0, 0), axis=dim)
 
 
 def rms_scale(values, scale_gain):
@@ -97,7 +102,7 @@
     slot_rank = jnp.sum((jnp.cumsum(slot_hits, axis=0) - slot_hits) * slot_hits, axis=1)
     copies_out = jnp.repeat(normed, route_count, axis=0)
     gate_up, down_proj = (
-        lax.all_gather(placed_gate_up, "shard", axis=1, tiled=True),
+        all_by_exchange(placed_gate_up, "shard", 1),
         lax.all_gather(placed_down, "shard", axis=1, tiled=True),
     )
     buffer_index = slot_ids * capacity + slot_rank

time: 299 us -> 369 us (1.23)
  waiting for transfers between devices: 199 us -> 255 us
  local copies, waits for them, and re-layouts: 23.9 us -> 32.3 us
  starting transfers between devices: 13.4 us -> 21.4 us
    all_gather x1 -> x0, waiting for transfers between devices: 55 us -> none  [body(): lax.all_gather(placed_gate_up, 'shard', axis=1, tiled=True)]
    all_gather x1, waiting for transfers between devices: 21.6 us -> 68.6 us  [body(): lax.all_gather(output_weight, 'shard', axis=0, tiled=True)]
    all_to_all x1, waiting for transfers between devices: 9.92 us -> 47.5 us  [body(): lax.all_to_all(outbound.reshape(groups, slot_count * capacity, model_widt...]
    all_to_all x0 -> x1, waiting for transfers between devices: none -> 15.4 us  [all_by_exchange(): return jnp.concatenate(lax.all_to_all(sent, axis, 0, 0), axis=dim)]
    all_gather x1, waiting for transfers between devices: 22.6 us -> 34.5 us  [body(): lax.all_gather(placed_down, 'shard', axis=1, tiled=True)]
    all_to_all x0 -> x1, starting transfers between devices: none -> 8.6 us  [all_by_exchange(): return jnp.concatenate(lax.all_to_all(sent, axis, 0, 0), axis=dim)]
    all_to_all x0 -> x1, local copies, waits for them, and re-layouts: none -> 4.82 us  [all_by_exchange(): return jnp.concatenate(lax.all_to_all(sent, axis, 0, 0), axis=dim)]
  transfers between devices with their start and end apart: 5 -> 5, of which waited for: 5 -> 5; matrix products, arithmetic and copies ran while one was open for 11% -> 10% of each run, Pallas kernels for 0% -> 0%
where the time goes in v1:
time: 369 us
  waiting for transfers between devices  255 us (69%)
  local copies, waits for them, and re-layouts  32.3 us (9%)
  matrix products  24.8 us (7%)
  starting transfers between devices  21.4 us (6%)
  other arithmetic  21.4 us (6%)
  between operations  13.6 us (4%)
    all_to_all x1, waiting for transfers between devices, body(): lax.all_to_all(answers.reshape(groups, slot_count * capacity, model_width...  87.8 us
    all_gather x1, waiting for transfers between devices, body(): lax.all_gather(output_weight, 'shard', axis=0, tiled=True)  68.6 us
    all_to_all x1, waiting for transfers between devices, body(): lax.all_to_all(outbound.reshape(groups, slot_count * capacity, model_widt...  47.5 us
    all_gather x1, waiting for transfers between devices, body(): lax.all_gather(placed_down, 'shard', axis=1, tiled=True)  34.5 us
    dot_general x4, matrix products, apply_block(): jnp.einsum('bjmd,jdf->bjmf', block_part, gate_up, preferred_element_type=...  18.4 us
    another operation x3, other arithmetic  18.2 us
    all_to_all x1, waiting for transfers between devices, all_by_exchange(): return jnp.concatenate(lax.all_to_all(sent, axis, 0, 0), axis=dim)  15.4 us
    scatter x1, local copies, waits for them, and re-layouts, body(): outbound = jnp.zeros((place_count * capacity, model_width), jnp.bfloat16)...  9.08 us
  transfers between devices with their start and end apart: 5, of which 5 were waited for; matrix products, arithmetic and copies ran while one was open for 10% of the time, Pallas kernels for 0%

profile of v1, /device:TPU:8, one launch (start us, length us, event | category | flops | bytes accessed | tf_op | source)
XLA Modules:
  0.0 368.8 jit_solution(10193764956387213659)
XLA Ops:
  6.5 3.5 stack.2
  10.1 8.6 %all-to-all-start.1 = ((bf16[8,2,128,1024]{3,2,1,0:T(8,128)(2,1)}), bf16[8,2,128,1024]{3,2,1,0:T(8,128)(2,1)}, u32[]{:S(2)}, u32[]{:S(2)}) async-start(bf16[8,2,128,1024]{3,2,1,0:T(8,128)(2,1)} %stack.2), calls=%async_computation.1 | async-start | bytes 8388608 | tf_op jit(solution)/shard_map/all_to_all | solution.py:14
  18.7 0.7 all-gather.3.cloned.1.call-update
  19.5 0.2 reduce_window_sum.26
  19.7 0.2 fusion.33
  19.8 0.1 select_reduce_fusion.3
  20.0 0.1 broadcast_multiply_fusion
  20.1 0.1 copy.44
  20.2 0.1 eq.111
  20.3 0.1 eq.107
  20.4 0.1 copy.43
  20.5 0.1 mul.172
  20.6 18.0 %reduce-window.6 = s32[64,8,128]{2,1,0:T(8,128)S(1)} reduce-window(s32[64,8,128]{2,1,0:T(8,128)S(1)} %fusion.27, s32[]{:T(128)} %copy.73), window={size=1x1x128 pad=0_0x0_0x127_0}, to_apply=%region_12.13 | reduce-window | flops 8323072 | bytes 524292 | tf_op jit(solution)/shard_map/reduce-window
  38.6 0.1 slice.18
  38.8 0.1 copy.46
  39.0 0.1 copy.47
  39.1 0.1 broadcast_add_fusion
  39.3 68.6 %all-gather.3.cloned.1.call-done = bf16[1024,1024]{1,0:T(8,128)(2,1)} async-done(((bf16[128,1024]{1,0:T(8,128)(2,1)}), bf16[1024,1024]{1,0:T(8,128)(2,1)}) %all-gather.3.cloned.1.call-update) | async-done | bytes 2097168 | tf_op jit(solution)/shard_map/all_gather | solution.py:88
  107.9 2.1 multiply_reduce_fusion.1
  110.0 0.1 multiply_convert_fusion.1
  110.1 9.1 %scatter_custom_fusion = bf16[3072,1024]{1,0:T(8,128)(2,1)} fusion(s32[1024]{0:T(1024)S(1)} %bitcast.79, bf16[]{:T(256)} %constant.52.clone.1, bf16[128,1024]{1,0:T(8,128)(2,1)S(1)} %multiply_convert_fusion.1), kind=kCustom, calls=%fused_computation.18 | custom fusion | bytes 6553602 | tf_op jit(solution)/shard_map/scatter | solution.py:112
  119.2 15.4 %all-to-all-done.1 = bf16[8,2,128,1024]{3,2,1,0:T(8,128)(2,1)} async-done(((bf16[8,2,128,1024]{3,2,1,0:T(8,128)(2,1)}), bf16[8,2,128,1024]{3,2,1,0:T(8,128)(2,1)}, u32[]{:S(2)}, u32[]{:S(2)}) %all-to-all-start.1) | async-done | bytes 4194336 | tf_op jit(solution)/shard_map/all_to_all | solution.py:14
  134.6 7.6 %all-to-all-start = ((bf16[32,96,1024]{2,1,0:T(8,128)(2,1)}), bf16[32,96,1024]{2,1,0:T(8,128)(2,1)}, u32[]{:S(2)}, u32[]{:S(2)}) async-start(bf16[32,96,1024]{2,1,0:T(8,128)(2,1)} %bitcast.73), calls=%async_computation | async-start | bytes 12582912 | tf_op jit(solution)/shard_map/all_to_all | solution.py:114
  142.3 0.7 all-gather.5.cloned.1.call-update
  143.0 4.8 %copy.48 = bf16[8,2,128,1024]{3,2,0,1:T(8,128)(2,1)} copy(bf16[8,2,128,1024]{3,2,1,0:T(8,128)(2,1)} %all-to-all-done.1) | data formatting | bytes 8388608 | tf_op jit(solution)/shard_map/all_to_all | solution.py:14
  147.8 34.5 %all-gather.5.cloned.1.call-done = bf16[2,512,1024]{2,1,0:T(8,128)(2,1)} async-done(((bf16[2,64,1024]{2,1,0:T(8,128)(2,1)}), bf16[2,512,1024]{2,1,0:T(8,128)(2,1)}) %all-gather.5.cloned.1.call-update) | async-done | bytes 2097168 | tf_op jit(solution)/shard_map/all_gather | solution.py:106
  182.3 47.5 %all-to-all-done = bf16[32,96,1024]{2,1,0:T(8,128)(2,1)} async-done(((bf16[32,96,1024]{2,1,0:T(8,128)(2,1)}), bf16[32,96,1024]{2,1,0:T(8,128)(2,1)}, u32[]{:S(2)}, u32[]{:S(2)}) %all-to-all-start) | async-done | bytes 6291488 | tf_op jit(solution)/shard_map/all_to_all | solution.py:114
  229.8 27.9 %while.10 = (s32[]{:T(128)}, bf16[4,8,2,48,1024]{4,3,2,1,0:T(8,128)(2,1)}, bf16[4,8,2,48,1024]{4,3,2,1,0:T(8,128)(2,1)}, bf16[2,1024,1024]{2,1,0:T(8,128)(2,1)}, bf16[2,512,1024]{2,1,0:T(8,128)(2,1)}, /*index=5*/s32[]{:T(128)}) while((s32[]{:T(128)}, bf16[4,8,2,48,1024]{4,3,2,1,0:T(8,128)(2,1)}, bf16[4,8,2,48,1024]{4,3,2,1,0:T(8,128)(2,1)}, ...), condition=%wide.region_17.18_spmd, body=%wide.region_16.17_spmd.sunk | while | flops 2419064832 | bytes 27263088 | solution.py:63
  229.8 4.6 %fusion.48 = f32[8,2,48,1024]{3,2,0,1:T(8,128)S(1)} fusion(bf16[2,1024,1024]{2,1,0:T(8,128)(2,1)} %get-tuple-element.123, bf16[4,8,2,48,1024]{4,3,2,1,0:T(8,128)(2,1)} %get-tuple-element.122, s32[]{:T(128)S(6)} %copy.68), kind=kOutput, calls=%fused_computation.6.clone.1 | convolution fusion | flops 1610612736 | bytes 8912900 | tf_op jit(solution)/shard_map/while/body/eval_jaxpr/bjmd,jdf->bjmf/dot_general | solution.py:53
  234.4 1.0 fusion.49
  235.5 1.4 copy_dynamic-update-slice_fusion.2
  236.8 4.6 %fusion.48 = f32[8,2,48,1024]{3,2,0,1:T(8,128)S(1)} fusion(bf16[2,1024,1024]{2,1,0:T(8,128)(2,1)} %get-tuple-element.123, bf16[4,8,2,48,1024]{4,3,2,1,0:T(8,128)(2,1)} %get-tuple-element.122, s32[]{:T(128)S(6)} %copy.68), kind=kOutput, calls=%fused_computation.6.clone.1 | convolution fusion | flops 1610612736 | bytes 8912900 | tf_op jit(solution)/shard_map/while/body/eval_jaxpr/bjmd,jdf->bjmf/dot_general | solution.py:53
  241.4 1.0 fusion.49
  242.5 1.3 copy_dynamic-update-slice_fusion.2
  243.8 4.6 %fusion.48 = f32[8,2,48,1024]{3,2,0,1:T(8,128)S(1)} fusion(bf16[2,1024,1024]{2,1,0:T(8,128)(2,1)} %get-tuple-element.123, bf16[4,8,2,48,1024]{4,3,2,1,0:T(8,128)(2,1)} %get-tuple-element.122, s32[]{:T(128)S(6)} %copy.68), kind=kOutput, calls=%fused_computation.6.clone.1 | convolution fusion | flops 1610612736 | bytes 8912900 | tf_op jit(solution)/shard_map/while/body/eval_jaxpr/bjmd,jdf->bjmf/dot_general | solution.py:53
  248.4 1.0 fusion.49
  249.4 1.3 copy_dynamic-update-slice_fusion.2
  250.7 4.6 %fusion.48 = f32[8,2,48,1024]{3,2,0,1:T(8,128)S(1)} fusion(bf16[2,1024,1024]{2,1,0:T(8,128)(2,1)} %get-tuple-element.123, bf16[4,8,2,48,1024]{4,3,2,1,0:T(8,128)(2,1)} %get-tuple-element.122, s32[]{:T(128)S(6)} %copy.68), kind=kOutput, calls=%fused_computation.6.clone.1 | convolution fusion | flops 1610612736 | bytes 8912900 | tf_op jit(solution)/shard_map/while/body/eval_jaxpr/bjmd,jdf->bjmf/dot_general | solution.py:53
  255.3 1.0 fusion.49
  256.4 1.4 copy_dynamic-update-slice_fusion.2
  257.7 5.1 %all-to-all-start.2 = ((bf16[32,96,1024]{2,1,0:T(8,128)(2,1)}), bf16[32,96,1024]{2,1,0:T(8,128)(2,1)}, u32[]{:S(2)}, u32[]{:S(2)}) async-start(bf16[32,96,1024]{2,1,0:T(8,128)(2,1)} %bitcast.74), calls=%async_computation.2 | async-start | bytes 12582912 | tf_op jit(solution)/shard_map/all_to_all | solution.py:123
  262.9 0.2 fusion.35
  263.2 0.1 copy.42
  263.3 87.8 %all-to-all-done.2 = bf16[32,96,1024]{2,1,0:T(8,128)(2,1)} async-done(((bf16[32,96,1024]{2,1,0:T(8,128)(2,1)}), bf16[32,96,1024]{2,1,0:T(8,128)(2,1)}, u32[]{:S(2)}, u32[]{:S(2)}) %all-to-all-start.2) | async-done | bytes 6291488 | tf_op jit(solution)/shard_map/all_to_all | solution.py:123
  351.1 8.6 %gather_fusion = bf16[1024,1024]{1,0:T(8,128)(2,1)S(1)} fusion(bf16[3072,1024]{1,0:T(8,128)(2,1)} %bitcast.18, s32[1024]{0:T(1024)S(1)} %broadcast_clamp_fusion), kind=kCustom, calls=%fused_computation | custom fusion | bytes 4198400 | tf_op jit(solution)/shard_map/gather | solution.py:131
  359.7 1.3 fusion.17
  361.0 0.2 multiply_reduce_fusion
  361.2 0.8 multiply_convert_fusion
  (39 shorter events, 0.4 us)
Async XLA Ops:
  6.5 101.3 %copy-start = (bf16[128,1024]{1,0:T(8,128)(2,1)S(1)}, bf16[128,1024]{1,0:T(8,128)(2,1)}, u32[]{:S(2)}) copy-start(bf16[128,1024]{1,0:T(8,128)(2,1)} %param.13) | copy-start | bytes 786436
  10.1 9.3 %copy-start.7 = (s32[64]{0:T(128)S(1)}, s32[64]{0:T(128)}, u32[]{:S(2)}) copy-start(s32[64]{0:T(128)} %param.22) | copy-start | bytes 772
  10.1 9.7 %copy-start.3 = (s32[128,8]{0,1:T(8,128)S(1)}, s32[128,8]{0,1:T(8,128)}, u32[]{:S(2)}) copy-start(s32[128,8]{0,1:T(8,128)} %param.20) | copy-start | bytes 12292
  10.1 9.9 %copy-start.6 = (s32[128,8]{0,1:T(8,128)S(1)}, s32[128,8]{0,1:T(8,128)}, u32[]{:S(2)}) copy-start(s32[128,8]{0,1:T(8,128)} %param.21) | copy-start | bytes 12292
  10.1 124.5 %all-to-all-start.1 = ((bf16[8,2,128,1024]{3,2,1,0:T(8,128)(2,1)}), bf16[8,2,128,1024]{3,2,1,0:T(8,128)(2,1)}, u32[]{:S(2)}, u32[]{:S(2)}) async-start(bf16[8,2,128,1024]{3,2,1,0:T(8,128)(2,1)} %stack.2), calls=%async_computation.1 | async-start | bytes 8388608 | tf_op jit(solution)/shard_map/all_to_all | solution.py:14
  18.7 89.2 %copy-start.1 = (bf16[128,1024]{1,0:T(8,128)(2,1)S(1)}, bf16[128,1024]{1,0:T(8,128)(2,1)}, u32[]{:S(2)}) copy-start(bf16[128,1024]{1,0:T(8,128)(2,1)} %param.14) | copy-start | bytes 786436
  18.7 89.2 %all-gather.3.cloned.1.call-start = ((), (), s32[]{:S(2)}) async-start(), calls=%async_computation.3 | async-start | bytes 2359296 | tf_op jit(solution)/shard_map/all_gather | solution.py:88
  38.8 71.2 %copy-start.4 = (f32[1024]{0:T(1024)S(1)}, f32[1024]{0:T(1024)}, u32[]{:S(2)}) copy-start(f32[1024]{0:T(1024)} %param.17) | copy-start | bytes 12292
  134.6 95.2 %all-to-all-start = ((bf16[32,96,1024]{2,1,0:T(8,128)(2,1)}), bf16[32,96,1024]{2,1,0:T(8,128)(2,1)}, u32[]{:S(2)}, u32[]{:S(2)}) async-start(bf16[32,96,1024]{2,1,0:T(8,128)(2,1)} %bitcast.73), calls=%async_computation | async-start | bytes 12582912 | tf_op jit(solution)/shard_map/all_to_all | solution.py:114
  142.2 40.0 %all-gather.5.cloned.1.call-start = ((), (), s32[]{:S(2)}) async-start(), calls=%async_computation.4 | async-start | bytes 2359296 | tf_op jit(solution)/shard_map/all_gather | solution.py:106
  229.8 4.6 %copy-start.8 = (bf16[2,512,1024]{2,1,0:T(8,128)(2,1)S(1)}, bf16[2,512,1024]{2,1,0:T(8,128)(2,1)}, u32[]{:S(2)}) copy-start(bf16[2,512,1024]{2,1,0:T(8,128)(2,1)} %get-tuple-element.124) | copy-start | bytes 6291460 | tf_op jit(solution)/shard_map/while
  236.8 4.6 %copy-start.8 = (bf16[2,512,1024]{2,1,0:T(8,128)(2,1)S(1)}, bf16[2,512,1024]{2,1,0:T(8,128)(2,1)}, u32[]{:S(2)}) copy-start(bf16[2,512,1024]{2,1,0:T(8,128)(2,1)} %get-tuple-element.124) | copy-start | bytes 6291460 | tf_op jit(solution)/shard_map/while
  243.8 4.6 %copy-start.8 = (bf16[2,512,1024]{2,1,0:T(8,128)(2,1)S(1)}, bf16[2,512,1024]{2,1,0:T(8,128)(2,1)}, u32[]{:S(2)}) copy-start(bf16[2,512,1024]{2,1,0:T(8,128)(2,1)} %get-tuple-element.124) | copy-start | bytes 6291460 | tf_op jit(solution)/shard_map/while
  250.7 4.6 %copy-start.8 = (bf16[2,512,1024]{2,1,0:T(8,128)(2,1)S(1)}, bf16[2,512,1024]{2,1,0:T(8,128)(2,1)}, u32[]{:S(2)}) copy-start(bf16[2,512,1024]{2,1,0:T(8,128)(2,1)} %get-tuple-element.124) | copy-start | bytes 6291460 | tf_op jit(solution)/shard_map/while
  257.7 5.1 %copy-start.2 = (bf16[1024,32]{0,1:T(8,128)(2,1)S(1)}, bf16[1024,32]{0,1:T(8,128)(2,1)}, u32[]{:S(2)}) copy-start(bf16[1024,32]{0,1:T(8,128)(2,1)} %param.16) | copy-start | bytes 196612
  257.7 93.3 %all-to-all-start.2 = ((bf16[32,96,1024]{2,1,0:T(8,128)(2,1)}), bf16[32,96,1024]{2,1,0:T(8,128)(2,1)}, u32[]{:S(2)}, u32[]{:S(2)}) async-start(bf16[32,96,1024]{2,1,0:T(8,128)(2,1)} %bitcast.74), calls=%async_computation.2 | async-start | bytes 12582912 | tf_op jit(solution)/shard_map/all_to_all | solution.py:123
  359.7 1.5 copy-start.5
Sparse Core Ops, SparseCore 0:
  21.3 86.5 all-gather.2
  144.8 37.3 all-gather.4
